TPU v7x, 256 devices: a whole 4x4x8 slice. The times are simulated.
256 devices in a mesh: fsdp: 16 (over y_lo, z), dp: 16 (over x, y_hi, core).
Axes of the slice: x: 4, y: 4 (y_hi: 2, y_lo: 2; y = y_hi * 2 + y_lo), z: 8, core: 2. Of those that a mesh axis runs over, the one named last changes fastest.
Arguments:
- patch_acts: bfloat16 [32768, 12288], P(('fsdp', 'dp')), may hold values from -6 to 6
- patch_slot: int32 [32768], P(('fsdp', 'dp')), may hold values from 0 to 1024, as said below
- out_grads: bfloat16 [16384, 3072], P(('fsdp', 'dp')), may hold values from -6 to 6
- latent_weight: bfloat16 [12288, 3072], P('dp', 'fsdp'), may hold values from -0.0546875 to 0.0546875
- step_size: bfloat16 [1, 3072], P(None, 'fsdp')
Outputs:
- grad_acts: bfloat16 [32768, 12288], P(('fsdp', 'dp'))
- grad_weight: float32 [12288, 3072], P('dp', 'fsdp')
- grad_step: float32 [1, 3072], P(None, 'fsdp')
Inputs may be any that keep to these rules, and one draw needn't show every extreme that they name: `patch_slot`: within each fsdp index, the used patch rows of every image owner come first in its 128 slots and carry a packed row below 1024, the others carry 1024; each packed row of the fsdp index receives exactly one patch row; in every fsdp index some image owner has all 128 slots used.
All inputs are finite; a program needn't handle non-finite values.
Results may differ from a plain program's by a relative error of at most 0.0049.
Values may be sent and summed in bfloat16 or wider, within the bound.
No kernel may reach another device: no remote copies, remote signals or barrier semaphores. Data moves between devices by JAX's collectives and lax.ppermute only.
A program may use at most 128 MiB of HBM per device.

v0:
```python
import jax
import jax.numpy as jnp
from jax import lax
from jax.sharding import PartitionSpec as P

FF_W = 12288
top_level = 7.0
wobble = 0.9
two_pi = 6.283185307179586
inv_root_two = 0.7071067811865476
inv_root_tau = 0.3989422804014327


def gelu_pair(values):
    normal_cdf = 0.5 * (1.0 + jax.scipy.special.erf(values * inv_root_two))
    density = jnp.exp(-0.5 * values * values) * inv_root_tau
    return (values * normal_cdf, normal_cdf + values * density)


def soft_quantize(weight, step):
    ratio = weight / step
    clipped = top_level * jnp.tanh(ratio / top_level)
    phase = two_pi * clipped
    quantized = clipped - wobble * jnp.sin(phase) / two_pi
    slope = (1.0 - wobble * jnp.cos(phase)) * (1.0 - clipped / top_level * (clipped / top_level))
    return (quantized, slope, ratio)


def contract_last(left, right):
    return lax.dot_general(
        left, right, (((1,), (1,)), ((), ())), preferred_element_type=jnp.float32
    )


def contract_first(left, right):
    return lax.dot_general(
        left, right, (((0,), (0,)), ((), ())), preferred_element_type=jnp.float32
    )


def shards(patch_acts, patch_slot, out_grads, latent_weight, step_size):
    dp_count = lax.axis_size("dp")
    capacity, features = patch_acts.shape
    hidden = features // dp_count
    packed_rows = out_grads.shape[0] * dp_count
    outgoing = patch_acts.reshape(capacity, dp_count, hidden)
    labels = jnp.broadcast_to(patch_slot[:, None], (capacity, dp_count))
    incoming, slot_labels = (
        lax.all_to_all(outgoing, "dp", split_axis=1, concat_axis=0, tiled=True),
        lax.all_to_all(labels, "dp", split_axis=1, concat_axis=0, tiled=True),
    )
    incoming = incoming.reshape(dp_count * capacity, hidden)
    slot_labels = slot_labels.reshape(dp_count * capacity)
    holder = jnp.zeros((packed_rows + 1, hidden), jnp.bfloat16).at[slot_labels].set(incoming)
    packed = holder[:packed_rows]
    act_full, gelu_slope = gelu_pair(packed.astype(jnp.float32))
    act = act_full.astype(jnp.bfloat16)
    full_grads = lax.all_gather(out_grads, "dp", axis=0, tiled=True)
    step_local = step_size.astype(jnp.float32)
    quantized, slope, ratio = soft_quantize(latent_weight.astype(jnp.float32), step_local)
    step_piece = lax.all_gather(step_size, "fsdp", axis=1, tiled=True).astype(jnp.float32)
    piece_quant, piece_slope, piece_ratio = soft_quantize(
        lax.all_gather(latent_weight, "fsdp", axis=1, tiled=True).astype(jnp.float32), step_piece
    )
    piece_weight = (step_piece * piece_quant).astype(jnp.bfloat16)
    columns = full_grads
    grad_hidden = contract_last(columns, piece_weight)
    grad_packed = (grad_hidden * gelu_slope).astype(jnp.bfloat16)
    padded = jnp.concatenate([grad_packed, jnp.zeros((1, hidden), jnp.bfloat16)], axis=0)
    picked = jnp.take(padded, slot_labels, axis=0).reshape(dp_count * capacity, 1, hidden)
    returned = lax.all_to_all(picked, "dp", split_axis=0, concat_axis=1, tiled=True)
    grad_acts = returned.reshape(capacity, features)
    columns = full_grads
    grad_qweight = lax.psum_scatter(
        contract_first(columns, act), "fsdp", scatter_dimension=0, tiled=True
    ).T
    grad_weight = grad_qweight * slope
    partial_step = jnp.sum(grad_qweight * (quantized - ratio * slope), axis=0, keepdims=True)
    scale_factor = (FF_W * top_level) ** (-0.5)
    grad_step = scale_factor * lax.psum(partial_step, "dp")
    return (grad_acts, grad_weight, grad_step)


def solution(mesh):
    return jax.shard_map(
        shards,
        mesh=mesh,
        in_specs=(
            P(("fsdp", "dp"), None),
            P(("fsdp", "dp")),
            P(("fsdp", "dp"), None),
            P("dp", "fsdp"),
            P(None, "fsdp"),
        ),
        out_specs=(P(("fsdp", "dp"), None), P("dp", "fsdp"), P(None, "fsdp")),
        check_vma=False,
    )
```

profile of v0, /device:TPU:8, one launch (start us, length us, event | category | flops | bytes accessed | tf_op | source)
XLA Modules:
  0.0 394.6 jit_solution(10012122353420767556)
XLA Ops:
  7.2 0.0 all-gather.5.cloned.1.call-start
  7.2 0.7 all-gather.5.cloned.1.call-update
  7.9 0.0 all-gather.3.cloned.1.call-start
  7.9 0.7 all-gather.3.cloned.1.call-update
  8.6 1.3 broadcast_in_dim.24
  9.9 6.1 %all-to-all-start = ((s32[128,16,1]{0,2,1:T(1,128)}), s32[128,16,1]{0,2,1:T(1,128)S(1)}, u32[]{:S(2)}, u32[]{:S(2)}) async-start(s32[128,16,1]{0,2,1:T(1,128)} %broadcast_in_dim.24), calls=%async_computation | async-start | bytes 16384 | tf_op jit(solution)/shard_map/all_to_all | solution.py:50
  16.1 3.5 copy.35
  19.5 2.8 copy.36
  22.3 1.2 all-to-all-done
  23.5 6.0 %all-to-all-start.1 = ((bf16[128,16,768]{2,0,1:T(8,128)(2,1)}), bf16[128,16,768]{2,0,1:T(8,128)(2,1)S(1)}, u32[]{:S(2)}, u32[]{:S(2)}) async-start(bf16[128,16,768]{2,0,1:T(8,128)(2,1)} %copy.36), calls=%async_computation.1 | async-start | bytes 6291456 | tf_op jit(solution)/shard_map/all_to_all | solution.py:49
  29.5 0.0 reduce-scatter.4.cloned.1.call-start
  29.6 50.0 %all-to-all-done.1 = bf16[128,16,768]{2,0,1:T(8,128)(2,1)S(1)} async-done(((bf16[128,16,768]{2,0,1:T(8,128)(2,1)}), bf16[128,16,768]{2,0,1:T(8,128)(2,1)S(1)}, u32[]{:S(2)}, u32[]{:S(2)}) %all-to-all-start.1) | async-done | bytes 3145760 | tf_op jit(solution)/shard_map/all_to_all | solution.py:49
  79.6 0.0 copy-start
  79.6 1.7 copy-done
  81.3 10.6 %scatter_custom_fusion = bf16[1025,768]{1,0:T(8,128)(2,1)S(1)} fusion(s32[2048]{0:T(1024)S(1)} %bitcast.43, bf16[2048,768]{1,0:T(8,128)(2,1)} %bitcast.41, bf16[]{:T(256)} %constant.16.clone.1), kind=kCustom, calls=%fused_computation.20 | custom fusion | bytes 1574912 | tf_op jit(solution)/shard_map/scatter | solution.py:54
  91.9 0.1 slice.6
  92.0 0.8 copy.47
  92.7 6.3 %all-gather.5.cloned.1.call-done = bf16[1024,3072]{1,0:T(8,128)(2,1)} async-done(((bf16[64,3072]{1,0:T(8,128)(2,1)}), bf16[1024,3072]{1,0:T(8,128)(2,1)}) %all-gather.5.cloned.1.call-update) | async-done | bytes 6291472 | tf_op jit(solution)/shard_map/all_gather | solution.py:58
  99.1 10.2 %convolution_bitcast_fusion = f32[3072,768]{0,1:T(8,128)} fusion(bf16[1024,3072]{1,0:T(8,128)(2,1)} %all-gather.5.cloned.1.call-done, bf16[1024,768]{0,1:T(8,128)(2,1)S(1)} %copy.47), kind=kOutput, calls=%fused_computation.8 | convolution fusion | flops 4836556800 | bytes 17301504 | tf_op jit(solution)/shard_map/dot_general | solution.py:36
  109.2 9.6 %copy.44 = f32[3072,768]{1,0:T(8,128)} copy(f32[3072,768]{0,1:T(8,128)} %convolution_bitcast_fusion) | data formatting | bytes 18874368
  118.9 0.0 copy-start.2
  118.9 0.0 reduce-scatter.4.cloned.1.call-update
  118.9 0.6 copy-done.2
  119.5 0.6 dynamic-slice
  120.8 0.0 copy-done.1
  120.8 0.2 dynamic-update-slice
  121.1 35.8 %all-reduce.1 = bf16[3072]{0:T(1024)(128)(2,1)S(1)} all-reduce(bf16[3072]{0:T(1024)(128)(2,1)S(1)} %dynamic-update-slice), channel_id=1, replica_groups=mesh['fsdp'=16,'dp'=16] {'fsdp'}, use_global_device_ids=true, to_apply=%add.1 | all-reduce | flops 3072 | bytes 12288
  156.9 23.6 %all-gather.3.cloned.1.call-done = bf16[768,3072]{0,1:T(8,128)(2,1)} async-done(((bf16[768,192]{0,1:T(8,128)(2,1)}), bf16[768,3072]{0,1:T(8,128)(2,1)}) %all-gather.3.cloned.1.call-update) | async-done | bytes 4718608 | tf_op jit(solution)/shard_map/all_gather | solution.py:63
  180.6 44.4 %fusion.8 = bf16[1024,768]{0,1:T(8,128)(2,1)} fusion(bf16[1024,768]{0,1:T(8,128)(2,1)S(1)} %copy.47, bf16[1024,3072]{1,0:T(8,128)(2,1)} %all-gather.5.cloned.1.call-done, bf16[768,3072]{0,1:T(8,128)(2,1)} %all-gather.3.cloned.1.call-done, f32[3072]{0:T(1024)S(1)} %mul.123), kind=kOutput, calls=%fused_computation.17 | convolution fusion | flops 4861722624 | bytes 14168064 | tf_op jit(solution)/shard_map/dot_general | solution.py:30
  225.0 1.7 copy.48
  226.7 0.1 concatenate.3.clone
  226.8 9.4 %gather_fusion = bf16[2048,768]{1,0:T(8,128)(2,1)} fusion(bf16[1025,768]{1,0:T(8,128)(2,1)S(1)} %concatenate.3.clone, s32[2048]{0:T(1024)S(1)} %broadcast_clamp_fusion), kind=kCustom, calls=%fused_computation | custom fusion | bytes 6299648 | tf_op jit(solution)/shard_map/jit(_take)/gather | solution.py:70
  236.2 2.2 bitcast_select_fusion
  238.4 0.5 broadcast.113
  238.9 3.7 reduce.2
  242.6 6.4 %reshape.124 = bf16[16,2,49152]{2,1,0:T(2,128)(2,1)} reshape(bf16[2048,768]{1,0:T(8,128)(2,1)} %reduce.2) | data formatting | bytes 6291456
  249.0 5.9 %all-to-all-start.2 = ((bf16[16,2,49152]{2,1,0:T(2,128)(2,1)}), bf16[16,2,49152]{2,1,0:T(2,128)(2,1)S(1)}, u32[]{:S(2)}, u32[]{:S(2)}) async-start(bf16[16,2,49152]{2,1,0:T(2,128)(2,1)} %reshape.124), calls=%async_computation.2 | async-start | bytes 6291456 | tf_op jit(solution)/shard_map/all_to_all | solution.py:71
  254.9 1.1 copy.41
  256.1 70.4 %all-to-all-done.2 = bf16[16,2,49152]{2,1,0:T(2,128)(2,1)S(1)} async-done(((bf16[16,2,49152]{2,1,0:T(2,128)(2,1)}), bf16[16,2,49152]{2,1,0:T(2,128)(2,1)S(1)}, u32[]{:S(2)}, u32[]{:S(2)}) %all-to-all-start.2) | async-done | bytes 3145760 | tf_op jit(solution)/shard_map/all_to_all | solution.py:71
  326.4 7.7 %reshape.125 = bf16[2048,1,768]{2,1,0:T(2,128)(2,1)} reshape(bf16[16,2,49152]{2,1,0:T(2,128)(2,1)S(1)} %all-to-all-done.2) | data formatting | bytes 6291456
  334.1 5.0 %copy.46 = bf16[2048,1,768]{2,0,1:T(8,128)(2,1)} copy(bf16[2048,1,768]{2,1,0:T(2,128)(2,1)} %reshape.125) | data formatting | bytes 6291456
  339.1 3.5 copy.40
  342.6 2.8 copy.42
  345.4 1.3 copy.45
  346.7 3.3 fusion.13
  350.0 1.1 copy.43
  351.1 36.4 %psum.7 = f32[1,192]{1,0:T(1,128)S(1)} all-reduce(f32[1,192]{1,0:T(1,128)S(1)} %bitcast.46), channel_id=1, replica_groups=mesh['fsdp'=16,'dp'=16] {'dp'}, use_global_device_ids=true, to_apply=%region_3.4 | all-reduce | flops 192 | bytes 1536 | tf_op jit(solution)/shard_map/psum | solution.py:80
  387.5 0.6 broadcast_multiply_fusion
  (8 shorter events, 0.1 us)
Async XLA Ops:
  7.2 91.9 %all-gather.5.cloned.1.call-start = ((), (), s32[]{:S(2)}) async-start(), calls=%async_computation.5 | async-start | bytes 6684672 | tf_op jit(solution)/shard_map/all_gather | solution.py:58
  7.9 172.7 %all-gather.3.cloned.1.call-start = ((), (), s32[]{:S(2)}) async-start(), calls=%async_computation.4 | async-start | bytes 5013504 | tf_op jit(solution)/shard_map/all_gather | solution.py:63
  9.9 13.6 %all-to-all-start = ((s32[128,16,1]{0,2,1:T(1,128)}), s32[128,16,1]{0,2,1:T(1,128)S(1)}, u32[]{:S(2)}, u32[]{:S(2)}) async-start(s32[128,16,1]{0,2,1:T(1,128)} %broadcast_in_dim.24), calls=%async_computation | async-start | bytes 16384 | tf_op jit(solution)/shard_map/all_to_all | solution.py:50
  23.5 56.1 %all-to-all-start.1 = ((bf16[128,16,768]{2,0,1:T(8,128)(2,1)}), bf16[128,16,768]{2,0,1:T(8,128)(2,1)S(1)}, u32[]{:S(2)}, u32[]{:S(2)}) async-start(bf16[128,16,768]{2,0,1:T(8,128)(2,1)} %copy.36), calls=%async_computation.1 | async-start | bytes 6291456 | tf_op jit(solution)/shard_map/all_to_all | solution.py:49
  29.5 315.8 %reduce-scatter.4.cloned.1.call-start = ((), (), s32[]{:S(2)}) async-start(), calls=%async_computation.6 | async-start | bytes 10027008
  79.6 1.7 copy-start
  118.9 0.7 copy-start.2
  118.9 1.9 copy-start.1
  249.0 77.5 %all-to-all-start.2 = ((bf16[16,2,49152]{2,1,0:T(2,128)(2,1)}), bf16[16,2,49152]{2,1,0:T(2,128)(2,1)S(1)}, u32[]{:S(2)}, u32[]{:S(2)}) async-start(bf16[16,2,49152]{2,1,0:T(2,128)(2,1)} %reshape.124), calls=%async_computation.2 | async-start | bytes 6291456 | tf_op jit(solution)/shard_map/all_to_all | solution.py:71
Sparse Core Ops, SparseCore 0:
  10.7 88.3 all-gather.4
  100.8 79.6 all-gather.2
  183.1 130.3 reduce-scatter.3
where the time goes:
time: 395 us
  waiting for transfers between devices  153 us (39%)
  local copies, waits for them, and re-layouts  72.3 us (18%)
  blocking collectives  72.2 us (18%)
  matrix products  54.6 us (14%)
  starting transfers between devices  18.2 us (5%)
  between operations  14.6 us (4%)
  other arithmetic  9.8 us (2%)
    all_to_all x1, waiting for transfers between devices, shards(): lax.all_to_all(picked, 'dp', split_axis=0, concat_axis=1, tiled=True)  70.4 us
    all_to_all x1, waiting for transfers between devices, shards(): lax.all_to_all(outgoing, 'dp', split_axis=1, concat_axis=0, tiled=True)  50 us
    dot_general x1, matrix products, contract_last(): lax.dot_general(left, right, (((1,), (1,)), ((), ())), preferred_element_...  44.4 us
    unnamed x20, local copies, waits for them, and re-layouts  44.1 us
    psum x1, blocking collectives, shards(): grad_step = scale_factor * lax.psum(partial_step, 'dp')  36.4 us
    unnamed x1, blocking collectives  35.8 us
    all_gather x1, waiting for transfers between devices, shards(): lax.all_gather(latent_weight, 'fsdp', axis=1, tiled=True)  23.6 us
    scatter x1, local copies, waits for them, and re-layouts, shards(): jnp.zeros((packed_rows + 1, hidden), jnp.bfloat16).at[slot_labels]  10.6 us
  transfers between devices with their start and end apart: 6, of which 5 were waited for; matrix products, arithmetic and copies ran while one was open for 32% of the time, Pallas kernels for 0%

commit v1 on v0

--- a/solution.py
+++ b/solution.py
@@ -9,6 +9,11 @@
 two_pi = 6.283185307179586
 inv_root_two = 0.7071067811865476
 inv_root_tau = 0.3989422804014327
+
+
+def step_on_ways(patch):
+    small = lax.all_gather(patch, axis_name="dp").sum(axis=0)
+    return small
 
 
 def gelu_pair(values):
@@ -77,7 +82,7 @@
     grad_weight = grad_qweight * slope
     partial_step = jnp.sum(grad_qweight * (quantized - ratio * slope), axis=0, keepdims=True)
     scale_factor = (FF_W * top_level) ** (-0.5)
-    grad_step = scale_factor * lax.psum(partial_step, "dp")
+    grad_step = scale_factor * step_on_ways(partial_step)
     return (grad_acts, grad_weight, grad_step)
 
 

time: 395 us -> 427 us (1.081)
  blocking collectives: 72.2 us -> 104 us
    unnamed x1 -> x2, blocking collectives: 35.8 us -> 104 us
    psum x1 -> x0, blocking collectives: 36.4 us -> none  [shards(): grad_step = scale_factor * lax.psum(partial_step, 'dp')]
    unnamed x20 -> x25, local copies, waits for them, and re-layouts: 44.1 us -> 44.9 us
  transfers between devices with their start and end apart: 6 -> 6, of which waited for: 5 -> 5; matrix products, arithmetic and copies ran while one was open for 32% -> 30% of each run, Pallas kernels for 0% -> 0%
where the time goes in v1:
time: 427 us; the launch traced here: 426 us
  waiting for transfers between devices  151 us (35%)
  blocking collectives  104 us (24%)
  local copies, waits for them, and re-layouts  73.2 us (17%)
  matrix products  54.6 us (13%)
  starting transfers between devices  18.6 us (4%)
  between operations  15.2 us (4%)
  other arithmetic  9.84 us (2%)
    unnamed x2, blocking collectives  104 us
    all_to_all x1, waiting for transfers between devices, shards(): lax.all_to_all(picked, 'dp', split_axis=0, concat_axis=1, tiled=True)  68.6 us
    all_to_all x1, waiting for transfers between devices, shards(): lax.all_to_all(outgoing, 'dp', split_axis=1, concat_axis=0, tiled=True)  50 us
    unnamed x25, local copies, waits for them, and re-layouts  44.9 us
    dot_general x1, matrix products, contract_last(): lax.dot_general(left, right, (((1,), (1,)), ((), ())), preferred_element_...  44.4 us
    all_gather x1, waiting for transfers between devices, shards(): lax.all_gather(latent_weight, 'fsdp', axis=1, tiled=True)  23.7 us
    scatter x1, local copies, waits for them, and re-layouts, shards(): jnp.zeros((packed_rows + 1, hidden), jnp.bfloat16).at[slot_labels]  10.6 us
    dot_general x1, matrix products, contract_first(): lax.dot_general(left, right, (((0,), (0,)), ((), ())), preferred_element_...  10.2 us
  transfers between devices with their start and end apart: 6, of which 5 were waited for; matrix products, arithmetic and copies ran while one was open for 30% of the time, Pallas kernels for 0%

profile of v1, /device:TPU:8, one launch (start us, length us, event | category | flops | bytes accessed | tf_op | source)
XLA Modules:
  0.0 426.5 jit_solution(13572323326055705115)
XLA Ops:
  7.2 0.0 all-gather.6.cloned.1.call-start
  7.2 0.7 all-gather.6.cloned.1.call-update
  7.9 0.0 all-gather.4.cloned.1.call-start
  7.9 0.7 all-gather.4.cloned.1.call-update
  8.6 1.3 broadcast_in_dim.21
  9.9 6.1 %all-to-all-start = ((s32[128,16,1]{0,2,1:T(1,128)}), s32[128,16,1]{0,2,1:T(1,128)S(1)}, u32[]{:S(2)}, u32[]{:S(2)}) async-start(s32[128,16,1]{0,2,1:T(1,128)} %broadcast_in_dim.21), calls=%async_computation | async-start | bytes 16384 | tf_op jit(solution)/shard_map/all_to_all | solution.py:55
  16.1 3.5 copy.45
  19.5 2.8 copy.46
  22.3 1.2 all-to-all-done
  23.5 6.0 %all-to-all-start.1 = ((bf16[128,16,768]{2,0,1:T(8,128)(2,1)}), bf16[128,16,768]{2,0,1:T(8,128)(2,1)S(1)}, u32[]{:S(2)}, u32[]{:S(2)}) async-start(bf16[128,16,768]{2,0,1:T(8,128)(2,1)} %copy.46), calls=%async_computation.1 | async-start | bytes 6291456 | tf_op jit(solution)/shard_map/all_to_all | solution.py:54
  29.5 0.0 reduce-scatter.4.cloned.1.call-start
  29.6 50.0 %all-to-all-done.1 = bf16[128,16,768]{2,0,1:T(8,128)(2,1)S(1)} async-done(((bf16[128,16,768]{2,0,1:T(8,128)(2,1)}), bf16[128,16,768]{2,0,1:T(8,128)(2,1)S(1)}, u32[]{:S(2)}, u32[]{:S(2)}) %all-to-all-start.1) | async-done | bytes 3145760 | tf_op jit(solution)/shard_map/all_to_all | solution.py:54
  79.6 1.7 copy-done
  81.3 10.6 %scatter_custom_fusion = bf16[1025,768]{1,0:T(8,128)(2,1)S(1)} fusion(s32[2048]{0:T(1024)S(1)} %bitcast.44, bf16[2048,768]{1,0:T(8,128)(2,1)} %bitcast.42, bf16[]{:T(256)} %constant.16.clone.1), kind=kCustom, calls=%fused_computation.20 | custom fusion | bytes 1574912 | tf_op jit(solution)/shard_map/scatter | solution.py:59
  91.9 0.1 slice.6
  92.0 0.8 copy.57
  92.7 6.3 %all-gather.6.cloned.1.call-done = bf16[1024,3072]{1,0:T(8,128)(2,1)} async-done(((bf16[64,3072]{1,0:T(8,128)(2,1)}), bf16[1024,3072]{1,0:T(8,128)(2,1)}) %all-gather.6.cloned.1.call-update) | async-done | bytes 6291472 | tf_op jit(solution)/shard_map/all_gather | solution.py:63
  99.1 10.2 %convolution_bitcast_fusion = f32[3072,768]{0,1:T(8,128)} fusion(bf16[1024,3072]{1,0:T(8,128)(2,1)} %all-gather.6.cloned.1.call-done, bf16[1024,768]{0,1:T(8,128)(2,1)S(1)} %copy.57), kind=kOutput, calls=%fused_computation.8 | convolution fusion | flops 4836556800 | bytes 17301504 | tf_op jit(solution)/shard_map/dot_general | solution.py:41
  109.2 9.6 %copy.54 = f32[3072,768]{1,0:T(8,128)} copy(f32[3072,768]{0,1:T(8,128)} %convolution_bitcast_fusion) | data formatting | bytes 18874368
  118.9 0.0 reduce-scatter.4.cloned.1.call-update
  118.9 0.6 copy-done.3
  119.5 0.6 dynamic-slice
  120.8 0.2 dynamic-update-slice
  121.1 35.8 %all-reduce.1 = bf16[3072]{0:T(1024)(128)(2,1)S(1)} all-reduce(bf16[3072]{0:T(1024)(128)(2,1)S(1)} %dynamic-update-slice), channel_id=1, replica_groups=mesh['fsdp'=16,'dp'=16] {'fsdp'}, use_global_device_ids=true, to_apply=%add.1 | all-reduce | flops 3072 | bytes 12288
  157.0 23.7 %all-gather.4.cloned.1.call-done = bf16[768,3072]{0,1:T(8,128)(2,1)} async-done(((bf16[768,192]{0,1:T(8,128)(2,1)}), bf16[768,3072]{0,1:T(8,128)(2,1)}) %all-gather.4.cloned.1.call-update) | async-done | bytes 4718608 | tf_op jit(solution)/shard_map/all_gather | solution.py:68
  180.6 44.4 %fusion.8 = bf16[1024,768]{0,1:T(8,128)(2,1)} fusion(bf16[1024,768]{0,1:T(8,128)(2,1)S(1)} %copy.57, bf16[1024,3072]{1,0:T(8,128)(2,1)} %all-gather.6.cloned.1.call-done, bf16[768,3072]{0,1:T(8,128)(2,1)} %all-gather.4.cloned.1.call-done, f32[3072]{0:T(1024)S(1)} %mul.135), kind=kOutput, calls=%fused_computation.17 | convolution fusion | flops 4861722624 | bytes 14168064 | tf_op jit(solution)/shard_map/dot_general | solution.py:35
  225.0 1.7 copy.58
  226.8 0.1 concatenate.3.clone
  226.9 9.4 %gather_fusion = bf16[2048,768]{1,0:T(8,128)(2,1)} fusion(bf16[1025,768]{1,0:T(8,128)(2,1)S(1)} %concatenate.3.clone, s32[2048]{0:T(1024)S(1)} %broadcast_clamp_fusion), kind=kCustom, calls=%fused_computation | custom fusion | bytes 6299648 | tf_op jit(solution)/shard_map/jit(_take)/gather | solution.py:75
  236.3 2.2 bitcast_select_fusion
  238.5 0.5 broadcast.124
  239.0 3.7 reduce.4
  242.7 6.4 %reshape.142 = bf16[16,2,49152]{2,1,0:T(2,128)(2,1)} reshape(bf16[2048,768]{1,0:T(8,128)(2,1)} %reduce.4) | data formatting | bytes 6291456
  249.0 6.3 %all-to-all-start.2 = ((bf16[16,2,49152]{2,1,0:T(2,128)(2,1)}), bf16[16,2,49152]{2,1,0:T(2,128)(2,1)S(1)}, u32[]{:S(2)}, u32[]{:S(2)}) async-start(bf16[16,2,49152]{2,1,0:T(2,128)(2,1)} %reshape.142), calls=%async_computation.2 | async-start | bytes 6291456 | tf_op jit(solution)/shard_map/all_to_all | solution.py:76
  255.4 1.1 copy.51
  256.5 0.6 dynamic-slice.1
  257.8 68.6 %all-to-all-done.2 = bf16[16,2,49152]{2,1,0:T(2,128)(2,1)S(1)} async-done(((bf16[16,2,49152]{2,1,0:T(2,128)(2,1)}), bf16[16,2,49152]{2,1,0:T(2,128)(2,1)S(1)}, u32[]{:S(2)}, u32[]{:S(2)}) %all-to-all-start.2) | async-done | bytes 3145760 | tf_op jit(solution)/shard_map/all_to_all | solution.py:76
  326.4 7.6 %reshape.143 = bf16[2048,1,768]{2,1,0:T(2,128)(2,1)} reshape(bf16[16,2,49152]{2,1,0:T(2,128)(2,1)S(1)} %all-to-all-done.2) | data formatting | bytes 6291456
  334.1 5.0 %copy.56 = bf16[2048,1,768]{2,0,1:T(8,128)(2,1)} copy(bf16[2048,1,768]{2,1,0:T(2,128)(2,1)} %reshape.143) | data formatting | bytes 6291456
  339.0 3.5 copy.50
  342.5 2.8 copy.52
  345.3 1.3 copy.55
  346.6 3.3 fusion.13
  349.9 0.3 dynamic-update-slice.1
  350.2 68.0 %all-reduce.2 = f32[3072]{0:T(1024)S(1)} all-reduce(f32[3072]{0:T(1024)S(1)} %dynamic-update-slice.1), channel_id=2, replica_groups=mesh['fsdp'=16,'dp'=16] {'dp'}, use_global_device_ids=true, to_apply=%add.2 | all-reduce | flops 3072 | bytes 24576
  418.2 0.1 reshape.123
  418.3 0.6 broadcast_multiply_fusion
  418.9 1.1 copy.53
  (15 shorter events, 0.1 us)
Async XLA Ops:
  7.2 91.9 %all-gather.6.cloned.1.call-start = ((), (), s32[]{:S(2)}) async-start(), calls=%async_computation.5 | async-start | bytes 6684672 | tf_op jit(solution)/shard_map/all_gather | solution.py:63
  7.9 172.7 %all-gather.4.cloned.1.call-start = ((), (), s32[]{:S(2)}) async-start(), calls=%async_computation.4 | async-start | bytes 5013504 | tf_op jit(solution)/shard_map/all_gather | solution.py:68
  9.9 13.6 %all-to-all-start = ((s32[128,16,1]{0,2,1:T(1,128)}), s32[128,16,1]{0,2,1:T(1,128)S(1)}, u32[]{:S(2)}, u32[]{:S(2)}) async-start(s32[128,16,1]{0,2,1:T(1,128)} %broadcast_in_dim.21), calls=%async_computation | async-start | bytes 16384 | tf_op jit(solution)/shard_map/all_to_all | solution.py:55
  23.5 56.1 %all-to-all-start.1 = ((bf16[128,16,768]{2,0,1:T(8,128)(2,1)}), bf16[128,16,768]{2,0,1:T(8,128)(2,1)S(1)}, u32[]{:S(2)}, u32[]{:S(2)}) async-start(bf16[128,16,768]{2,0,1:T(8,128)(2,1)} %copy.46), calls=%async_computation.1 | async-start | bytes 6291456 | tf_op jit(solution)/shard_map/all_to_all | solution.py:54
  29.5 315.7 %reduce-scatter.4.cloned.1.call-start = ((), (), s32[]{:S(2)}) async-start(), calls=%async_computation.6 | async-start | bytes 10027008
  79.6 1.7 copy-start
  118.9 0.7 copy-start.3
  118.9 1.9 copy-start.1
  249.0 7.5 %copy-start.2 = (u32[256]{0:T(256)S(1)}, u32[256]{0:T(256)}, u32[]{:S(2)}) copy-start(u32[256]{0:T(256)} %constant.69) | copy-start | bytes 3076
  249.0 77.4 %all-to-all-start.2 = ((bf16[16,2,49152]{2,1,0:T(2,128)(2,1)}), bf16[16,2,49152]{2,1,0:T(2,128)(2,1)S(1)}, u32[]{:S(2)}, u32[]{:S(2)}) async-start(bf16[16,2,49152]{2,1,0:T(2,128)(2,1)} %reshape.142), calls=%async_computation.2 | async-start | bytes 6291456 | tf_op jit(solution)/shard_map/all_to_all | solution.py:76
Sparse Core Ops, SparseCore 0:
  10.7 88.3 all-gather.5
  100.8 79.7 all-gather.3
  183.2 130.2 reduce-scatter.3
